TPU v7x, 256 devices: a whole 4x4x8 slice. The times are simulated.
256 devices in a mesh: wide: 64 (over y, x, z_lo), narrow: 4 (over z_hi, core).
Axes of the slice: x: 4, y: 4, z: 8 (z_hi: 2, z_lo: 4; z = z_hi * 4 + z_lo), core: 2. Of those that a mesh axis runs over, the one named last changes fastest.
Arguments:
- volume: float32 [1024, 48, 1024], P('wide', None, 'narrow'), may hold values from 0 to 2
- codes_in: bfloat16 [1024, 72, 1536], P('wide', None, 'narrow'), may hold values from -4 to 4
- x_transform: float32 [1024, 1024], replicated, may hold values from -1 to 1, as said below
- y_atoms: bfloat16 [1024, 1536], replicated, may hold values from -0.1875 to 0.1875
- de_atoms: bfloat16 [48, 72], replicated, may hold values from -0.875 to 0.875
Outputs:
- codes_out: bfloat16 [1024, 72, 1536], P('wide', None, 'narrow')
- estimate: bfloat16 [1024, 48, 1024], P('wide', None, 'narrow')
Inputs may be any that keep to these rules, and one draw needn't show every extreme that they name: x_transform is orthonormal: its transpose is its inverse.
All inputs are finite; a program needn't handle non-finite values.
Results may differ from a plain program's by a relative error of at most 0.0065.
Values may be sent and summed in bfloat16 or wider, within the bound.
A program may use at most 64 MiB of HBM per device.

v0:
```python
import jax
import jax.numpy as jnp
from jax import lax
from jax.sharding import PartitionSpec as P

step_size = 0.06
threshold = 0.05
best = lax.Precision.HIGHEST


def shards(volume, codes_in, x_transform, y_atoms, de_atoms):
    xrows, depth, ylocal = volume.shape
    klocal = codes_in.shape[2]
    where = lax.axis_index("narrow")
    y_rows = lax.dynamic_slice_in_dim(y_atoms, where * ylocal, ylocal, 0)
    y_cols = lax.dynamic_slice_in_dim(y_atoms, where * klocal, klocal, 1)
    de_wide = de_atoms.astype(jnp.float32)

    def apply_x(columns, forward):
        if forward:
            return jnp.dot(x_transform, columns, precision=best)
        return lax.dot_general(x_transform, columns, (((0,), (0,)), ((), ())), precision=best)

    def along_x(field, forward):
        flat = field.reshape(xrows, depth * ylocal)
        columns = lax.all_to_all(flat, "wide", split_axis=1, concat_axis=0, tiled=True)
        mixed = apply_x(columns, forward)
        returned = lax.all_to_all(mixed, "wide", split_axis=0, concat_axis=1, tiled=True)
        return returned.reshape(xrows, depth, ylocal)

    def rebuild(codes):
        atoms = jnp.einsum(
            "fk,bkc->bfc", de_atoms, codes, preferred_element_type=jnp.float32
        ).astype(jnp.bfloat16)
        return jnp.einsum(
            "bfc,yc->bfy",
            lax.all_gather(atoms, "narrow", axis=2, tiled=True),
            y_rows,
            preferred_element_type=jnp.float32,
        )

    target = along_x(volume, True)
    codes = codes_in
    misfit = rebuild(codes) - target
    pulled = jnp.einsum("fk,bfy->bky", de_wide, misfit, precision=best).astype(jnp.bfloat16)
    grads = jnp.einsum(
        "bky,yc->bkc",
        lax.all_gather(pulled, "narrow", axis=2, tiled=True),
        y_cols,
        preferred_element_type=jnp.float32,
    )
    moved = codes.astype(jnp.float32) - step_size * grads
    codes = (moved - jnp.clip(moved, -threshold, threshold)).astype(jnp.bfloat16)
    image = rebuild(codes)
    estimate = jnp.maximum(along_x(image, False), 0.0).astype(jnp.bfloat16)
    return (codes, estimate)


def solution(mesh):
    return jax.shard_map(
        shards,
        mesh=mesh,
        in_specs=(P("wide", None, "narrow"), P("wide", None, "narrow"), P(), P(), P()),
        out_specs=(P("wide", None, "narrow"), P("wide", None, "narrow")),
        check_vma=False,
    )
```

profile of v0, /device:TPU:1, one launch (start us, length us, event | category | flops | bytes accessed | tf_op | source)
XLA Modules:
  0.0 301.2 jit_solution(1969324107720229944)
XLA Ops:
  7.2 0.0 all-gather.4.cloned.1.call-start
  7.2 2.5 fusion.2
  9.7 0.0 all-gather.4.cloned.1.call-update
  9.7 2.5 all_to_all.48
  12.2 2.0 copy.14
  14.2 66.0 %all_to_all.64 = f32[16,64,192]{2,0,1:T(8,128)S(1)} all-to-all(f32[16,64,192]{2,0,1:T(8,128)S(1)} %copy.14), channel_id=1, replica_groups=mesh['wide'=64,'narrow'=4] {'wide'}, dimensions={1} | all-to-all | bytes 1572864 | tf_op jit(solution)/shard_map/all_to_all | solution.py:26
  80.3 4.4 %fusion.18 = f32[64,16,192]{2,1,0:T(8,128)} fusion(f32[64,16,1024]{2,1,0:T(8,128)S(1)} %bitcast.46, f32[1024,192,1]{1,0,2:T(8,128)S(1)} %bitcast.47), kind=kOutput, calls=%fused_computation.25 | convolution fusion | flops 2415919104 | bytes 5767168 | tf_op jit(solution)/shard_map/dot_general | solution.py:21
  84.6 5.6 %all-to-all-start.1 = ((f32[64,16,192]{2,1,0:T(8,128)}), f32[64,16,192]{2,1,0:T(8,128)}, u32[]{:S(2)}, u32[]{:S(2)}) async-start(f32[64,16,192]{2,1,0:T(8,128)} %fusion.18), calls=%async_computation.1 | async-start | bytes 2097152 | tf_op jit(solution)/shard_map/all_to_all | solution.py:28
  90.3 0.0 all-gather.6.cloned.1.call-start
  90.3 28.1 %all-to-all-done.1 = f32[64,16,192]{2,1,0:T(8,128)} async-done(((f32[64,16,192]{2,1,0:T(8,128)}), f32[64,16,192]{2,1,0:T(8,128)}, u32[]{:S(2)}, u32[]{:S(2)}) %all-to-all-start.1) | async-done | bytes 786464 | tf_op jit(solution)/shard_map/all_to_all | solution.py:28
  118.5 2.8 copy.16
  121.3 2.7 reshape.30
  124.0 2.7 convolution_subtract_fusion
  126.7 1.5 fusion.1
  128.2 0.0 all-gather.6.cloned.1.call-update
  128.2 0.2 all-gather.8.cloned.1.call-start
  128.4 45.1 %all-gather.6.cloned.1.call-done = bf16[16,72,1024]{2,1,0:T(8,128)(2,1)} async-done(((bf16[16,72,256]{2,1,0:T(8,128)(2,1)}), bf16[16,72,1024]{2,1,0:T(8,128)(2,1)}) %all-gather.6.cloned.1.call-update) | async-done | bytes 2359312 | tf_op jit(solution)/shard_map/all_gather | solution.py:48
  173.5 3.3 %fusion = bf16[16,72,384]{2,1,0:T(8,128)(2,1)S(1)} fusion(bf16[16,72,384]{2,1,0:T(8,128)(2,1)} %param.6, bf16[16,72,1024]{2,1,0:T(8,128)(2,1)} %all-gather.6.cloned.1.call-done, bf16[1024,1536]{1,0:T(8,128)(2,1)S(1)} %copy-done, s32[]{:T(128)S(6)} %select_n.7), kind=kOutput, calls=%fused_computation.1 | convolution fusion | flops 908623872 | bytes 4915204 | tf_op jit(solution)/shard_map/bky,yc->bkc/dot_general | solution.py:46
  176.9 0.9 copy-done.3
  177.8 1.1 fusion.3
  179.0 0.0 all-gather.8.cloned.1.call-update
  179.0 42.3 %all-gather.8.cloned.1.call-done = bf16[16,48,1536]{2,1,0:T(8,128)(2,1)} async-done(((bf16[16,48,384]{2,1,0:T(8,128)(2,1)}), bf16[16,48,1536]{2,1,0:T(8,128)(2,1)}) %all-gather.8.cloned.1.call-update) | async-done | bytes 2359312 | tf_op jit(solution)/shard_map/all_gather | solution.py:37
  221.3 3.4 %fusion.5 = f32[16,48,256]{2,1,0:T(8,128)} fusion(bf16[16,48,1536]{2,1,0:T(8,128)(2,1)} %all-gather.8.cloned.1.call-done, bf16[1024,1536]{1,0:T(8,128)(2,1)S(1)} %copy-done, s32[]{:T(128)S(6)} %select_n.6), kind=kOutput, calls=%fused_computation.12 | convolution fusion | flops 603979776 | bytes 3932164 | tf_op jit(solution)/shard_map/bfc,yc->bfy/dot_general | solution.py:35
  224.7 2.5 all_to_all.54
  227.2 2.0 copy.17
  229.2 35.8 %all_to_all.65 = f32[16,64,192]{2,0,1:T(8,128)S(1)} all-to-all(f32[16,64,192]{2,0,1:T(8,128)S(1)} %copy.17), channel_id=1, replica_groups=mesh['wide'=64,'narrow'=4] {'wide'}, dimensions={1} | all-to-all | bytes 1572864 | tf_op jit(solution)/shard_map/all_to_all | solution.py:26
  265.0 3.0 convolution_bitcast_fusion
  268.0 1.0 copy.18
  269.0 22.1 %all_to_all.66 = bf16[64,16,192]{2,1,0:T(8,128)(2,1)S(1)} all-to-all(bf16[64,16,192]{2,1,0:T(8,128)(2,1)} %bitcast.49), channel_id=1, replica_groups=mesh['wide'=64,'narrow'=4] {'wide'}, dimensions={0} | all-to-all | bytes 786432 | tf_op jit(solution)/shard_map/all_to_all | solution.py:28
  291.1 0.1 fusion.11
  291.2 0.9 copy.19
  292.1 2.5 convert_element_type.44
  (10 shorter events, 0.0 us)
Async XLA Ops:
  7.2 116.9 %copy-start = (bf16[1024,1536]{1,0:T(8,128)(2,1)S(1)}, bf16[1024,1536]{1,0:T(8,128)(2,1)}, u32[]{:S(2)}) copy-start(bf16[1024,1536]{1,0:T(8,128)(2,1)} %param.8) | copy-start | bytes 9437188
  7.2 116.8 %all-gather.4.cloned.1.call-start = ((), (), s32[]{:S(2)}) async-start(), calls=%async_computation.4 | async-start | bytes 2949120 | tf_op jit(solution)/shard_map/all_gather | solution.py:37
  12.2 68.0 %copy-start.1 = (f32[1024,1024]{1,0:T(8,128)S(1)}, f32[1024,1024]{1,0:T(8,128)}, u32[]{:S(2)}) copy-start(f32[1024,1024]{1,0:T(8,128)} %param.7) | copy-start | bytes 12582916
  84.6 33.8 %all-to-all-start.1 = ((f32[64,16,192]{2,1,0:T(8,128)}), f32[64,16,192]{2,1,0:T(8,128)}, u32[]{:S(2)}, u32[]{:S(2)}) async-start(f32[64,16,192]{2,1,0:T(8,128)} %fusion.18), calls=%async_computation.1 | async-start | bytes 2097152 | tf_op jit(solution)/shard_map/all_to_all | solution.py:28
  90.3 83.3 %all-gather.6.cloned.1.call-start = ((), (), s32[]{:S(2)}) async-start(), calls=%async_computation.5 | async-start | bytes 2949120 | tf_op jit(solution)/shard_map/all_gather | solution.py:48
  124.0 2.7 copy-start.4
  128.2 93.1 %all-gather.8.cloned.1.call-start = ((), (), s32[]{:S(2)}) async-start(), calls=%async_computation.6 | async-start | bytes 2949120 | tf_op jit(solution)/shard_map/all_gather | solution.py:37
  176.9 0.9 copy-start.3
  227.2 37.8 %copy-start.2 = (f32[1024,1024]{1,0:T(8,128)S(1)}, f32[1024,1024]{1,0:T(8,128)}, u32[]{:S(2)}) copy-start(f32[1024,1024]{1,0:T(8,128)} %param.7) | copy-start | bytes 12582916
Sparse Core Ops, SparseCore 0:
  9.8 60.9 all-gather.3
  128.3 45.1 all-gather.5
  179.1 42.1 all-gather.7
where the time goes:
time: 302 us; the launch traced here: 301 us
  blocking collectives  124 us (41%)
  waiting for transfers between devices  116 us (38%)
  matrix products  21.8 us (7%)
  local copies, waits for them, and re-layouts  19.9 us (7%)
  between operations  13.8 us (5%)
  starting transfers between devices  5.94 us (2%)
    all_to_all x2, blocking collectives, along_x(): lax.all_to_all(flat, 'wide', split_axis=1, concat_axis=0, tiled=True)  102 us
    all_gather x1, waiting for transfers between devices, shards(): lax.all_gather(pulled, 'narrow', axis=2, tiled=True)  45.1 us
    all_gather x2, waiting for transfers between devices, rebuild(): lax.all_gather(atoms, 'narrow', axis=2, tiled=True)  42.3 us
    all_to_all x1, waiting for transfers between devices, along_x(): lax.all_to_all(mixed, 'wide', split_axis=0, concat_axis=1, tiled=True)  28.1 us
    all_to_all x1, blocking collectives, along_x(): lax.all_to_all(mixed, 'wide', split_axis=0, concat_axis=1, tiled=True)  22.1 us
    all_to_all x4, local copies, waits for them, and re-layouts, along_x(): lax.all_to_all(flat, 'wide', split_axis=1, concat_axis=0, tiled=True)  8.96 us
  transfers between devices with their start and end apart: 4, of which 3 were waited for; matrix products, arithmetic and copies ran while one was open for 4% of the time, Pallas kernels for 0%

commit v1 on v0

--- a/solution.py
+++ b/solution.py
@@ -45,7 +45,9 @@
     pulled = jnp.einsum("fk,bfy->bky", de_wide, misfit, precision=best).astype(jnp.bfloat16)
     grads = jnp.einsum(
         "bky,yc->bkc",
-        lax.all_gather(pulled, "narrow", axis=2, tiled=True),
+        jnp.concatenate(
+            lax.all_to_all(jnp.stack([pulled] * lax.axis_size("narrow")), "narrow", 0, 0), axis=2
+        ),
         y_cols,
         preferred_element_type=jnp.float32,
     )

time: 302 us -> 321 us (1.063)
  waiting for transfers between devices: 116 us -> 125 us
  starting transfers between devices: 5.94 us -> 14.5 us
  local copies, waits for them, and re-layouts: 19.9 us -> 23.5 us
    all_to_all x0 -> x1, waiting for transfers between devices: none -> 54.9 us  [shards(): lax.all_to_all(jnp.stack([pulled] * lax.axis_size('narrow')), 'narrow', 0...]
    all_gather x1 -> x0, waiting for transfers between devices: 45.1 us -> none  [shards(): lax.all_gather(pulled, 'narrow', axis=2, tiled=True)]
    all_to_all x0 -> x1, starting transfers between devices: none -> 8.84 us  [shards(): lax.all_to_all(jnp.stack([pulled] * lax.axis_size('narrow')), 'narrow', 0...]
where the time goes in v1:
time: 321 us; the launch traced here: 320 us
  waiting for transfers between devices  125 us (39%)
  blocking collectives  124 us (39%)
  local copies, waits for them, and re-layouts  23.5 us (7%)
  matrix products  19.2 us (6%)
  starting transfers between devices  14.5 us (5%)
  between operations  14.1 us (4%)
    all_to_all x2, blocking collectives, along_x(): lax.all_to_all(flat, 'wide', split_axis=1, concat_axis=0, tiled=True)  102 us
    all_to_all x1, waiting for transfers between devices, shards(): lax.all_to_all(jnp.stack([pulled] * lax.axis_size('narrow')), 'narrow', 0...  54.9 us
    all_gather x2, waiting for transfers between devices, rebuild(): lax.all_gather(atoms, 'narrow', axis=2, tiled=True)  41.8 us
    all_to_all x1, waiting for transfers between devices, along_x(): lax.all_to_all(mixed, 'wide', split_axis=0, concat_axis=1, tiled=True)  28.2 us
    all_to_all x1, blocking collectives, along_x(): lax.all_to_all(mixed, 'wide', split_axis=0, concat_axis=1, tiled=True)  22.1 us
    all_to_all x4, local copies, waits for them, and re-layouts, along_x(): lax.all_to_all(flat, 'wide', split_axis=1, concat_axis=0, tiled=True)  8.96 us
    all_to_all x1, starting transfers between devices, shards(): lax.all_to_all(jnp.stack([pulled] * lax.axis_size('narrow')), 'narrow', 0...  8.84 us
  transfers between devices with their start and end apart: 4, of which 3 were waited for; matrix products, arithmetic and copies ran while one was open for 4% of the time, Pallas kernels for 0%

profile of v1, /device:TPU:1, one launch (start us, length us, event | category | flops | bytes accessed | tf_op | source)
XLA Modules:
  0.0 320.2 jit_solution(7997671289831284637)
XLA Ops:
  7.2 0.0 all-gather.3.cloned.1.call-start
  7.2 2.5 fusion.2
  9.7 0.0 all-gather.3.cloned.1.call-update
  9.7 2.5 all_to_all.51
  12.2 2.0 copy.20
  14.2 66.0 %all_to_all.69 = f32[16,64,192]{2,0,1:T(8,128)S(1)} all-to-all(f32[16,64,192]{2,0,1:T(8,128)S(1)} %copy.20), channel_id=1, replica_groups=mesh['wide'=64,'narrow'=4] {'wide'}, dimensions={1} | all-to-all | bytes 1572864 | tf_op jit(solution)/shard_map/all_to_all | solution.py:26
  80.3 4.4 %fusion.18 = f32[64,16,192]{2,1,0:T(8,128)} fusion(f32[64,16,1024]{2,1,0:T(8,128)S(1)} %bitcast.49, f32[1024,192,1]{1,0,2:T(8,128)S(1)} %bitcast.50), kind=kOutput, calls=%fused_computation.25 | convolution fusion | flops 2415919104 | bytes 5767168 | tf_op jit(solution)/shard_map/dot_general | solution.py:21
  84.6 5.6 %all-to-all-start.1 = ((f32[64,16,192]{2,1,0:T(8,128)}), f32[64,16,192]{2,1,0:T(8,128)}, u32[]{:S(2)}, u32[]{:S(2)}) async-start(f32[64,16,192]{2,1,0:T(8,128)} %fusion.18), calls=%async_computation.1 | async-start | bytes 2097152 | tf_op jit(solution)/shard_map/all_to_all | solution.py:28
  90.3 28.2 %all-to-all-done.1 = f32[64,16,192]{2,1,0:T(8,128)} async-done(((f32[64,16,192]{2,1,0:T(8,128)}), f32[64,16,192]{2,1,0:T(8,128)}, u32[]{:S(2)}, u32[]{:S(2)}) %all-to-all-start.1) | async-done | bytes 786464 | tf_op jit(solution)/shard_map/all_to_all | solution.py:28
  118.5 2.8 copy.22
  121.3 2.7 reshape.38
  124.0 2.7 convolution_subtract_fusion
  126.7 0.7 fusion.1
  127.4 1.6 stack.2
  128.9 8.8 %all-to-all-start.2 = ((bf16[4,16,72,256]{3,2,1,0:T(8,128)(2,1)}), bf16[4,16,72,256]{3,2,1,0:T(8,128)(2,1)}, u32[]{:S(2)}, u32[]{:S(2)}) async-start(bf16[4,16,72,256]{3,2,1,0:T(8,128)(2,1)} %stack.2), calls=%async_computation.2 | async-start | bytes 4718592 | tf_op jit(solution)/shard_map/all_to_all | solution.py:49
  137.8 54.9 %all-to-all-done.2 = bf16[4,16,72,256]{3,2,1,0:T(8,128)(2,1)} async-done(((bf16[4,16,72,256]{3,2,1,0:T(8,128)(2,1)}), bf16[4,16,72,256]{3,2,1,0:T(8,128)(2,1)}, u32[]{:S(2)}, u32[]{:S(2)}) %all-to-all-start.2) | async-done | bytes 2359328 | tf_op jit(solution)/shard_map/all_to_all | solution.py:49
  192.6 2.1 copy.29
  194.7 1.5 fusion
  196.2 0.9 copy-done.4
  197.1 1.1 fusion.3
  198.3 0.0 all-gather.5.cloned.1.call-update
  198.3 41.8 %all-gather.5.cloned.1.call-done = bf16[16,48,1536]{2,1,0:T(8,128)(2,1)} async-done(((bf16[16,48,384]{2,1,0:T(8,128)(2,1)}), bf16[16,48,1536]{2,1,0:T(8,128)(2,1)}) %all-gather.5.cloned.1.call-update) | async-done | bytes 2359312 | tf_op jit(solution)/shard_map/all_gather | solution.py:37
  240.1 3.4 %fusion.5 = f32[16,48,256]{2,1,0:T(8,128)} fusion(bf16[16,48,1536]{2,1,0:T(8,128)(2,1)} %all-gather.5.cloned.1.call-done, bf16[1024,1536]{1,0:T(8,128)(2,1)S(1)} %copy-done, s32[]{:T(128)S(6)} %select_n.6), kind=kOutput, calls=%fused_computation.12 | convolution fusion | flops 603979776 | bytes 3932164 | tf_op jit(solution)/shard_map/bfc,yc->bfy/dot_general | solution.py:35
  243.5 2.5 all_to_all.58
  245.9 2.0 copy.24
  247.9 35.8 %all_to_all.70 = f32[16,64,192]{2,0,1:T(8,128)S(1)} all-to-all(f32[16,64,192]{2,0,1:T(8,128)S(1)} %copy.24), channel_id=1, replica_groups=mesh['wide'=64,'narrow'=4] {'wide'}, dimensions={1} | all-to-all | bytes 1572864 | tf_op jit(solution)/shard_map/all_to_all | solution.py:26
  283.7 3.0 convolution_bitcast_fusion
  286.7 1.0 copy.25
  287.7 22.1 %all_to_all.71 = bf16[64,16,192]{2,1,0:T(8,128)(2,1)S(1)} all-to-all(bf16[64,16,192]{2,1,0:T(8,128)(2,1)} %bitcast.53), channel_id=1, replica_groups=mesh['wide'=64,'narrow'=4] {'wide'}, dimensions={0} | all-to-all | bytes 786432 | tf_op jit(solution)/shard_map/all_to_all | solution.py:28
  309.8 0.1 fusion.11
  309.9 0.9 copy.26
  310.9 2.5 convert_element_type.44
  (13 shorter events, 0.0 us)
Async XLA Ops:
  7.2 116.9 %copy-start = (bf16[1024,1536]{1,0:T(8,128)(2,1)S(1)}, bf16[1024,1536]{1,0:T(8,128)(2,1)}, u32[]{:S(2)}) copy-start(bf16[1024,1536]{1,0:T(8,128)(2,1)} %param.8) | copy-start | bytes 9437188
  7.2 116.8 %all-gather.3.cloned.1.call-start = ((), (), s32[]{:S(2)}) async-start(), calls=%async_computation.5 | async-start | bytes 2949120 | tf_op jit(solution)/shard_map/all_gather | solution.py:37
  12.2 68.0 %copy-start.1 = (f32[1024,1024]{1,0:T(8,128)S(1)}, f32[1024,1024]{1,0:T(8,128)}, u32[]{:S(2)}) copy-start(f32[1024,1024]{1,0:T(8,128)} %param.7) | copy-start | bytes 12582916
  84.6 33.8 %all-to-all-start.1 = ((f32[64,16,192]{2,1,0:T(8,128)}), f32[64,16,192]{2,1,0:T(8,128)}, u32[]{:S(2)}, u32[]{:S(2)}) async-start(f32[64,16,192]{2,1,0:T(8,128)} %fusion.18), calls=%async_computation.1 | async-start | bytes 2097152 | tf_op jit(solution)/shard_map/all_to_all | solution.py:28
  124.0 2.7 copy-start.5
  128.9 63.7 %all-to-all-start.2 = ((bf16[4,16,72,256]{3,2,1,0:T(8,128)(2,1)}), bf16[4,16,72,256]{3,2,1,0:T(8,128)(2,1)}, u32[]{:S(2)}, u32[]{:S(2)}) async-start(bf16[4,16,72,256]{3,2,1,0:T(8,128)(2,1)} %stack.2), calls=%async_computation.2 | async-start | bytes 4718592 | tf_op jit(solution)/shard_map/all_to_all | solution.py:49
  137.8 102.3 %all-gather.5.cloned.1.call-start = ((), (), s32[]{:S(2)}) async-start(), calls=%async_computation.6 | async-start | bytes 2949120 | tf_op jit(solution)/shard_map/all_gather | solution.py:37
  192.6 2.1 copy-start.3
  196.2 0.9 copy-start.4
  245.9 37.8 %copy-start.2 = (f32[1024,1024]{1,0:T(8,128)S(1)}, f32[1024,1024]{1,0:T(8,128)}, u32[]{:S(2)}) copy-start(f32[1024,1024]{1,0:T(8,128)} %param.7) | copy-start | bytes 12582916
Sparse Core Ops, SparseCore 0:
  9.8 60.9 all-gather.2
  198.4 41.6 all-gather.4
